TPU v7x, 256 devices: a whole 4x4x8 slice. The times are simulated.
256 devices in a mesh: dp: 64 (over x, z_hi, y), tensor: 4 (over z_lo, core).
Axes of the slice: x: 4, y: 4, z: 8 (z_hi: 4, z_lo: 2; z = z_hi * 2 + z_lo), core: 2. Of those that a mesh axis runs over, the one named last changes fastest.
Arguments:
- tokens: bfloat16 [49152, 2048], P('dp'), may hold values from -6 to 6
- targets: bfloat16 [49152, 2048], P('dp'), may hold values from -6 to 6
- up_weight: bfloat16 [64, 64, 256, 256], P('dp', 'tensor'), may hold values from -6 to 6
- down_weight: bfloat16 [64, 64, 256, 256], P('dp', 'tensor'), may hold values from -6 to 6
- block_rows: int32 [64], P('tensor'), may hold values from 0 to 7, as said below
- block_columns: int32 [64], P('tensor'), may hold values from 0 to 7, as said below
Outputs:
- new_up: bfloat16 [64, 64, 256, 256], P('dp', 'tensor')
- new_down: bfloat16 [64, 64, 256, 256], P('dp', 'tensor')
- input_grad: bfloat16 [49152, 2048], P('dp', 'tensor')
Inputs may be any that keep to these rules, and one draw needn't show every extreme that they name: Within each tensor shard the 16 blocks sit at distinct (block_rows, block_columns) positions, and every hidden block of a shard holds exactly 2 of them; up_weight and down_weight share this pattern. `block_columns`: hidden block indices within a shard.
All inputs are finite; a program needn't handle non-finite values.
Results may differ from a plain program's by a relative error of at most 0.015.
Values may be sent and summed in bfloat16 or wider, within the bound.
A program may use at most 128 MiB of HBM per device.

v0:
```python
import jax
import jax.numpy as jnp
from jax import lax
from jax.experimental import pallas as pl
from jax.experimental.pallas import tpu as pltpu
from jax.sharding import PartitionSpec as P

D = 2048
H = 8192
STEP_RATE = 0.5
MESH = pl.DeviceIdType.MESH
F32 = jnp.float32
BF16 = jnp.bfloat16
TILE = 128
PIECE = 2
EARLY = (2, 2, 1)


def dot(a, b, contract):
    return lax.dot_general(a, b, (contract, ((), ())), preferred_element_type=F32)


NN = ((1,), (0,))
NT = ((1,), (1,))
TN = ((0,), (0,))


def sigmoid(v):
    return 1.0 / (1.0 + jnp.exp(-v))


def equal(a, b):
    return 1 - jnp.minimum((a - b) * (a - b), 1)


def less(a, b):
    return jnp.clip(b - a, 0, 1)


def rank_blocks(values_ref, rank_ref):
    n = values_ref.shape[0]

    @pl.loop(0, n)
    def _(k):
        own = values_ref[k] * n + k
        rank = jnp.int32(0)
        for j in range(n):
            rank += less(values_ref[j] * n + j, own)
        rank_ref[k] = rank


def in_order(rank_ref, value, place_ref):
    n = rank_ref.shape[0]

    @pl.loop(0, n)
    def _(i):
        place = jnp.int32(0)
        for k in range(n):
            place += value(k) * equal(rank_ref[k], i)
        place_ref[i] = place


def step_kernel(
    apart, scale_in, scale_out,
    rows_ref, cols_ref, tok_hbm, target_hbm, up_hbm, down_hbm,
    new_up_hbm, new_down_hbm, grad_hbm,
    tok, target, up, down, pre, act, dpre, seg, part, err_mine, err_other, gpart,
    out_twin, out_sum, out_across, grad_twin, grad_sum, grad_across, grad,
    peer, up_half, down_half,
    rank, col_block, col_row, row_block, row_col, row_row, keep, slot,
    load_sem, weight_sem, out_sem, grad_sem, store_sem,
):
    hidden, tok_count, block = pre.shape
    blocks = up.shape[0]
    model = tok.shape[0]
    half = tok_count // 2
    steps = half // TILE
    pieces = blocks // PIECE

    dp, t = lax.axis_index("dp"), lax.axis_index("tensor")
    twin, across, partner = (dp, t ^ 1), (dp, t ^ 2), (dp ^ (1 << apart), t)
    chip, core = t // 2, t % 2
    far = 1 - chip
    mine, other = core * half, (1 - core) * half

    def aligned(start):
        return pl.multiple_of(start, TILE)

    loads = [
        pltpu.make_async_copy(up_hbm, up, load_sem.at[0]),
        *(
            pltpu.make_async_copy(tok_hbm.at[:, b * block : (b + 1) * block], tok.at[b], load_sem.at[3 + b])
            for b in range(model)
        ),
        pltpu.make_async_copy(down_hbm, down, load_sem.at[1]),
        pltpu.make_async_copy(target_hbm.at[pl.ds(aligned(mine), half)], target, load_sem.at[2]),
    ]
    for load in loads:
        load.start()

    barrier = pltpu.get_barrier_semaphore()
    for device in (twin, across, partner):
        pl.semaphore_signal(barrier, inc=1, device_id=device, device_id_type=MESH)
    pl.semaphore_wait(barrier, 3)

    def remote(src, dst, sems, where, device):
        return pltpu.make_async_remote_copy(
            src_ref=src, dst_ref=dst, send_sem=sems.at[(0, *where)], recv_sem=sems.at[(1, *where)],
            device_id=device, device_id_type=MESH,
        )

    def weights_to_partner(which, p):
        span = pl.ds(p * PIECE, PIECE)
        return remote((up_hbm, down_hbm)[which].at[span], peer.at[which, span], weight_sem, (which, p), partner)

    everything = [(which, p) for which in range(2) for p in range(pieces)]

    def send_pieces(first, last):
        for which, p in everything[first:last]:
            weights_to_partner(which, p).start()

    cut = [sum(EARLY[: i + 1]) for i in range(3)]
    send_pieces(0, cut[0])

    rank_blocks(cols_ref, rank)
    in_order(rank, lambda k: k, col_block)
    in_order(rank, lambda k: rows_ref[k], col_row)
    rank_blocks(rows_ref, rank)
    in_order(rank, lambda k: k, row_block)
    in_order(rank, lambda k: cols_ref[k], row_col)
    in_order(rank, lambda k: rows_ref[k], row_row)
    keep[0] = 0

    @pl.loop(1, blocks)
    def _(j):
        keep[j] = equal(row_row[j], row_row[j - 1])

    @pl.loop(0, model)
    def _(b):
        upto, here = jnp.int32(0), jnp.int32(0)
        for k in range(blocks):
            upto += less(rows_ref[k], b + 1)
            here += equal(rows_ref[k], b)
        slot[b] = upto * jnp.minimum(here, 1)

    seg[0] = jnp.zeros_like(seg[0])
    for load in loads[:-1]:
        load.wait()

    def sum_by_row(left, right, contract, span):
        @pl.loop(0, blocks)
        def _(j):
            product = dot(left[row_col[j], span, :], right[row_block[j]], contract)
            seg[j + 1] = product + seg[j] * keep[j].astype(F32)

    def forward(base):
        span = pl.ds(aligned(base), TILE)

        @pl.loop(0, hidden)
        def _(h):
            first, second = (
                dot(tok[col_row[2 * h + i], span, :], up[col_block[2 * h + i]], NN) for i in range(2)
            )
            v = (first + second) * scale_in
            pre[h, span, :] = v
            act[h, span, :] = (v * sigmoid(v)).astype(BF16)

        sum_by_row(act, down, NN, span)
        for b in range(model):
            part[span, b * block : (b + 1) * block] = (seg[slot[b]] * scale_out).astype(BF16)

    def backward(base, err, i):
        span, near = pl.ds(aligned(base + i * TILE), TILE), pl.ds(aligned(i * TILE), TILE)

        @pl.loop(0, hidden)
        def _(h):
            first, second = (
                dot(err[col_row[2 * h + n], near, :], down[col_block[2 * h + n]], NT) for n in range(2)
            )
            dact = (first + second) * scale_out
            v = pre[h, span, :]
            sig = sigmoid(v)
            dpre[h, span, :] = (dact * sig * (1.0 + v * (1.0 - sig))).astype(BF16)

        sum_by_row(dpre, up, NT, span)
        per_owner = gpart.shape[2] // block
        for b in range(model):
            at = (b % per_owner) * block
            gpart[b // per_owner, span, at : at + block] = (seg[slot[b]] * scale_in).astype(BF16)

    def rows(base, i):
        return pl.ds(aligned(base + i * TILE), TILE)

    def part_to_twin(i):
        return remote(part.at[rows(other, i)], out_twin.at[rows(0, i)], out_sem, (0, i), twin)

    def sum_to_across(i):
        return remote(out_sum.at[rows(0, i)], out_across.at[rows(0, i)], out_sem, (1, i), across)

    def error_to_twin(i):
        return remote(err_mine.at[:, rows(0, i)], err_other.at[:, rows(0, i)], out_sem, (2, i), twin)

    def grad_to_twin(which, base, i):
        owner = (far, chip)[which]
        q = base // TILE + i
        return remote(
            gpart.at[2 * owner + 1 - core, rows(base, i)], grad_twin.at[which, rows(base, i)], grad_sem, (which, q), twin
        )

    def grad_to_across(base, i):
        q = base // TILE + i
        return remote(grad_sum.at[rows(base, i)], grad_across.at[rows(base, i)], grad_sem, (2, q), across)

    def strips(size, body):
        @pl.loop(0, TILE // size)
        def _(s):
            body(s * size)

    @pl.loop(0, steps)
    def _(i):
        forward(other + i * TILE)
        part_to_twin(i).start()

    @pl.loop(0, steps)
    def _(i):
        forward(mine + i * TILE)
        part_to_twin(i).wait_recv()

        def body(s):
            local = pl.ds(pl.multiple_of(i * TILE + s, 32), 32)
            whole = pl.ds(pl.multiple_of(mine + i * TILE + s, 32), 32)
            out_sum[local, :] = (part[whole, :].astype(F32) + out_twin[local, :].astype(F32)).astype(BF16)

        strips(32, body)
        sum_to_across(i).start()

    send_pieces(cut[0], cut[1])
    loads[-1].wait()

    @pl.loop(0, steps)
    def _(i):
        sum_to_across(i).wait_recv()

        def body(s):
            local = pl.ds(pl.multiple_of(i * TILE + s, 32), 32)
            output = out_sum[local, :].astype(F32) + out_across[local, :].astype(F32)
            error = (output - target[local, :].astype(F32)).astype(BF16)
            for b in range(model):
                err_mine[b, local, :] = error[:, b * block : (b + 1) * block]

        strips(32, body)
        error_to_twin(i).start()
        backward(mine, err_mine, i)
        grad_to_twin(0, mine, i).start()
        grad_to_twin(1, mine, i).start()

    send_pieces(cut[1], cut[2])

    @pl.loop(0, steps)
    def _(i):
        error_to_twin(i).wait_recv()

    def pass_on(base, i):
        grad_to_twin(0, base, i).wait_recv()

        def body(s):
            whole = pl.ds(pl.multiple_of(base + i * TILE + s, 64), 64)
            total = gpart[2 * far + core, whole, :].astype(F32) + grad_twin[0, whole, :].astype(F32)
            grad_sum[whole, :] = total.astype(BF16)

        strips(64, body)
        grad_to_across(base, i).start()

    def finish(base, i):
        grad_to_twin(1, base, i).wait_recv()
        grad_to_across(base, i).wait_recv()

        def body(s):
            whole = pl.ds(pl.multiple_of(base + i * TILE + s, 64), 64)
            total = gpart[2 * chip + core, whole, :].astype(F32) + grad_twin[1, whole, :].astype(F32)
            grad[whole, :] = (total + grad_across[whole, :].astype(F32)).astype(BF16)

        strips(64, body)

    @pl.loop(0, steps)
    def _(i):
        backward(other, err_other, i)
        grad_to_twin(0, other, i).start()
        grad_to_twin(1, other, i).start()
        pass_on(other, i)
        pass_on(mine, i)

    send_pieces(cut[2], len(everything))

    @pl.loop(0, blocks)
    def _(k):
        h = cols_ref[k]
        grad_down = dot(act[h, pl.ds(aligned(mine), half), :], err_mine[rows_ref[k]], TN)
        grad_down += dot(act[h, pl.ds(aligned(other), half), :], err_other[rows_ref[k]], TN)
        down_half[k] = 0.5 * down[k].astype(F32) - (STEP_RATE * scale_out) * grad_down
        grad_up = dot(tok[rows_ref[k]], dpre[h], TN)
        up_half[k] = 0.5 * up[k].astype(F32) - (STEP_RATE * scale_in) * grad_up

    @pl.loop(0, steps)
    def _(i):
        finish(other, i)
        finish(mine, i)

    store_grad = pltpu.make_async_copy(grad, grad_hbm, store_sem.at[2, 0])
    store_grad.start()

    for which, (own, held, new_hbm) in enumerate(((up, up_half, new_up_hbm), (down, down_half, new_down_hbm))):

        @pl.loop(0, pieces)
        def _(p):
            weights_to_partner(which, p).wait_recv()
            for b in range(PIECE):
                k = p * PIECE + b
                own[k] = (held[k] + 0.5 * peer[which, k].astype(F32)).astype(BF16)
            span = pl.ds(p * PIECE, PIECE)
            pltpu.make_async_copy(own.at[span], new_hbm.at[span], store_sem.at[which, p]).start()

    store_grad.wait()
    for which, (own, new_hbm) in enumerate(((up, new_up_hbm), (down, new_down_hbm))):

        @pl.loop(0, pieces)
        def _(p):
            weights_to_partner(which, p).wait_send()
            span = pl.ds(p * PIECE, PIECE)
            pltpu.make_async_copy(own.at[span], new_hbm.at[span], store_sem.at[which, p]).wait()

    @pl.loop(0, steps)
    def _(i):
        part_to_twin(i).wait_send()
        sum_to_across(i).wait_send()
        error_to_twin(i).wait_send()
        for base in (mine, other):
            grad_to_twin(0, base, i).wait_send()
            grad_to_twin(1, base, i).wait_send()
            grad_to_across(base, i).wait_send()


def on_device(tokens, targets, up_weight, down_weight, block_rows, block_columns):
    tok_count, width = tokens.shape
    up_local, down_local = up_weight[0], down_weight[0]
    blocks, block, _ = up_local.shape
    model = width // block
    tensor_count = lax.axis_size("tensor")
    hidden = H // (tensor_count * block)
    scale_in = (D // 4) ** (-0.5)
    scale_out = (H // 4) ** (-0.5)
    apart = (lax.axis_size("dp").bit_length() - 1) // 2
    half, owned = tok_count // 2, width // tensor_count
    steps, pieces = half // TILE, blocks // PIECE
    vmem, dma = pltpu.VMEM, pltpu.SemaphoreType.DMA
    anywhere = pl.BlockSpec(memory_space=pl.ANY)
    scalars = pl.BlockSpec(memory_space=pltpu.SMEM)
    weights = jax.ShapeDtypeStruct((blocks, block, block), BF16)
    flops = 12 * tok_count * blocks * block * block
    new_up, new_down, input_grad = pl.pallas_call(
        lambda *refs: step_kernel(apart, scale_in, scale_out, *refs),
        out_shape=[weights, weights, jax.ShapeDtypeStruct((tok_count, owned), BF16)],
        in_specs=[scalars, scalars, anywhere, anywhere, anywhere, anywhere],
        out_specs=[anywhere, anywhere, anywhere],
        scratch_shapes=[
            vmem((model, tok_count, block), BF16),
            vmem((half, width), BF16),
            vmem((blocks, block, block), BF16),
            vmem((blocks, block, block), BF16),
            vmem((hidden, tok_count, block), F32),
            vmem((hidden, tok_count, block), BF16),
            vmem((hidden, tok_count, block), BF16),
            vmem((blocks + 1, TILE, block), F32),
            vmem((tok_count, width), BF16),
            vmem((model, half, block), BF16),
            vmem((model, half, block), BF16),
            vmem((tensor_count, tok_count, owned), BF16),
            vmem((half, width), BF16),
            vmem((half, width), BF16),
            vmem((half, width), BF16),
            vmem((2, tok_count, owned), BF16),
            vmem((tok_count, owned), BF16),
            vmem((tok_count, owned), BF16),
            vmem((tok_count, owned), BF16),
            vmem((2, blocks, block, block), BF16),
            vmem((blocks, block, block), F32),
            vmem((blocks, block, block), F32),
            *[pltpu.SMEM((blocks,), jnp.int32)] * 7,
            pltpu.SMEM((model,), jnp.int32),
            dma((3 + model,)),
            dma((2, 2, pieces)),
            dma((2, 3, steps)),
            dma((2, 3, 2 * steps)),
            dma((3, pieces)),
        ],
        compiler_params=pltpu.CompilerParams(
            collective_id=0, has_side_effects=True, vmem_limit_bytes=62 << 20
        ),
        cost_estimate=pl.CostEstimate(flops=flops, bytes_accessed=20 << 20, transcendentals=0),
    )(block_rows, block_columns, tokens, targets, up_local, down_local)
    return (new_up[None], new_down[None], input_grad)


def solution(mesh):
    return jax.shard_map(
        on_device,
        mesh=mesh,
        in_specs=(
            P("dp", None),
            P("dp", None),
            P("dp", "tensor", None, None),
            P("dp", "tensor", None, None),
            P("tensor"),
            P("tensor"),
        ),
        out_specs=(P("dp", "tensor", None, None), P("dp", "tensor", None, None), P("dp", "tensor")),
        check_vma=False,
    )
```

profile of v0, /device:TPU:1, one launch (start us, length us, event | category | flops | bytes accessed | tf_op | source)
XLA Modules:
  0.0 252.8 jit_solution(14232095305554673060)
XLA Ops:
  0.6 246.3 %shard_map.85 = (bf16[16,256,256]{2,1,0:T(8,128)(2,1)}, bf16[16,256,256]{2,1,0:T(8,128)(2,1)}, bf16[768,512]{1,0:T(8,128)(2,1)}) custom-call(s32[16]{0:T(128)} %refs_0_.1, s32[16]{0:T(128)} %refs_1_.1, bf16[768,2048]{1,0:T(8,128)(2,1)} %refs_2_.1, bf16[768,2048]{1,0:T(8,128)(2,1)} %refs_3_.1, bf16[16,256,256]{2,1,0:T(8,128)(2,1)} %bitcast.6, ...), custom_call_target="tpu_custom_call" | custom-call | flops 9663676416 | bytes 20971520 | tf_op jit(solution)/shard_map/pallas_call | solution.py:360
  247.0 0.0 copy-start
  247.0 3.2 %copy.12 = bf16[1,16,256,256]{3,2,1,0:T(8,128)(2,1)} copy(bf16[1,16,256,256]{3,2,1,0:T(8,128)(2,1)} %bitcast.5) | data formatting | bytes 4194304
  250.2 0.0 copy-done
  250.2 0.0 copy-start.1
  250.2 1.3 copy.13
  251.5 0.4 copy-done.1
  251.9 0.9 copy.14
Async XLA Ops:
  247.0 3.3 %copy-start = (bf16[16,256,256]{2,1,0:T(8,128)(2,1)S(1)}, bf16[16,256,256]{2,1,0:T(8,128)(2,1)}, u32[]{:S(2)}) copy-start(bf16[16,256,256]{2,1,0:T(8,128)(2,1)} %get-tuple-element.7) | copy-start | bytes 6291460
  250.2 1.7 copy-start.1
where the time goes:
time: 253 us
  Pallas kernels  246 us (97%)
  local copies, waits for them, and re-layouts  5.8 us (2%)
    pallas_call x1, Pallas kernels, on_device(): pl.pallas_call(lambda *refs: step_kernel(apart, scale_in, scale_out, *ref...  246 us
    unnamed x7, local copies, waits for them, and re-layouts  5.8 us

commit v1 on v0

--- a/solution.py
+++ b/solution.py
@@ -13,7 +13,9 @@
 BF16 = jnp.bfloat16
 TILE = 128
 PIECE = 2
-EARLY = (2, 2, 1)
+VMEM_LIMIT = 54 << 20
+STORES = 4
+EARLY = (3, 3, 2)
 
 
 def dot(a, b, contract):
@@ -63,12 +65,12 @@
 def step_kernel(
     apart, scale_in, scale_out,
     rows_ref, cols_ref, tok_hbm, target_hbm, up_hbm, down_hbm,
-    new_up_hbm, new_down_hbm, grad_hbm,
+    new_up, new_down, grad,
     tok, target, up, down, pre, act, dpre, seg, part, err_mine, err_other, gpart,
-    out_twin, out_sum, out_across, grad_twin, grad_sum, grad_across, grad,
-    peer, up_half, down_half,
+    out_twin, out_sum, out_across, grad_twin, grad_sum, grad_across,
+    peer, down_half,
     rank, col_block, col_row, row_block, row_col, row_row, keep, slot,
-    load_sem, weight_sem, out_sem, grad_sem, store_sem,
+    load_sem, weight_sem, out_sem, grad_sem,
 ):
     hidden, tok_count, block = pre.shape
     blocks = up.shape[0]
@@ -188,6 +190,9 @@
             at = (b % per_owner) * block
             gpart[b // per_owner, span, at : at + block] = (seg[slot[b]] * scale_in).astype(BF16)
 
+    def up_half(k):
+        return pre.at[k // 2, pl.ds(pl.multiple_of((k % 2) * block, block), block)]
+
     def rows(base, i):
         return pl.ds(aligned(base + i * TILE), TILE)
 
@@ -299,35 +304,25 @@
         grad_down += dot(act[h, pl.ds(aligned(other), half), :], err_other[rows_ref[k]], TN)
         down_half[k] = 0.5 * down[k].astype(F32) - (STEP_RATE * scale_out) * grad_down
         grad_up = dot(tok[rows_ref[k]], dpre[h], TN)
-        up_half[k] = 0.5 * up[k].astype(F32) - (STEP_RATE * scale_in) * grad_up
+        up_half(k)[...] = 0.5 * up[k].astype(F32) - (STEP_RATE * scale_in) * grad_up
 
     @pl.loop(0, steps)
     def _(i):
         finish(other, i)
         finish(mine, i)
 
-    store_grad = pltpu.make_async_copy(grad, grad_hbm, store_sem.at[2, 0])
-    store_grad.start()
-
-    for which, (own, held, new_hbm) in enumerate(((up, up_half, new_up_hbm), (down, down_half, new_down_hbm))):
+    for which, (held, new) in enumerate(((up_half, new_up), (lambda k: down_half.at[k], new_down))):
 
         @pl.loop(0, pieces)
         def _(p):
             weights_to_partner(which, p).wait_recv()
             for b in range(PIECE):
                 k = p * PIECE + b
-                own[k] = (held[k] + 0.5 * peer[which, k].astype(F32)).astype(BF16)
-            span = pl.ds(p * PIECE, PIECE)
-            pltpu.make_async_copy(own.at[span], new_hbm.at[span], store_sem.at[which, p]).start()
-
-    store_grad.wait()
-    for which, (own, new_hbm) in enumerate(((up, new_up_hbm), (down, new_down_hbm))):
+                new[k] = (held(k)[...] + 0.5 * peer[which, k].astype(F32)).astype(BF16)
 
         @pl.loop(0, pieces)
         def _(p):
             weights_to_partner(which, p).wait_send()
-            span = pl.ds(p * PIECE, PIECE)
-            pltpu.make_async_copy(own.at[span], new_hbm.at[span], store_sem.at[which, p]).wait()
 
     @pl.loop(0, steps)
     def _(i):
@@ -338,6 +333,20 @@
             grad_to_twin(0, base, i).wait_send()
             grad_to_twin(1, base, i).wait_send()
             grad_to_across(base, i).wait_send()
+
+
+def store_kernel(*refs):
+    sources, targets, sems = refs[:3], refs[3:6], refs[6]
+    copies = []
+    for i, (source, target) in enumerate(zip(sources, targets)):
+        size = source.shape[0] // STORES
+        for j in range(STORES):
+            span = pl.ds(j * size, size)
+            copies.append(pltpu.make_async_copy(source.at[span], target.at[span], sems.at[i, j]))
+    for copy in copies:
+        copy.start()
+    for copy in copies:
+        copy.wait()
 
 
 def on_device(tokens, targets, up_weight, down_weight, block_rows, block_columns):
@@ -355,13 +364,13 @@
     vmem, dma = pltpu.VMEM, pltpu.SemaphoreType.DMA
     anywhere = pl.BlockSpec(memory_space=pl.ANY)
     scalars = pl.BlockSpec(memory_space=pltpu.SMEM)
-    weights = jax.ShapeDtypeStruct((blocks, block, block), BF16)
+    weights = vmem((blocks, block, block), BF16)
     flops = 12 * tok_count * blocks * block * block
     new_up, new_down, input_grad = pl.pallas_call(
         lambda *refs: step_kernel(apart, scale_in, scale_out, *refs),
-        out_shape=[weights, weights, jax.ShapeDtypeStruct((tok_count, owned), BF16)],
+        out_shape=[weights, weights, vmem((tok_count, owned), BF16)],
         in_specs=[scalars, scalars, anywhere, anywhere, anywhere, anywhere],
-        out_specs=[anywhere, anywhere, anywhere],
+        out_specs=[pl.BlockSpec(memory_space=vmem)] * 3,
         scratch_shapes=[
             vmem((model, tok_count, block), BF16),
             vmem((half, width), BF16),
@@ -381,9 +390,7 @@
             vmem((2, tok_count, owned), BF16),
             vmem((tok_count, owned), BF16),
             vmem((tok_count, owned), BF16),
-            vmem((tok_count, owned), BF16),
             vmem((2, blocks, block, block), BF16),
-            vmem((blocks, block, block), F32),
             vmem((blocks, block, block), F32),
             *[pltpu.SMEM((blocks,), jnp.int32)] * 7,
             pltpu.SMEM((model,), jnp.int32),
@@ -391,13 +398,21 @@
             dma((2, 2, pieces)),
             dma((2, 3, steps)),
             dma((2, 3, 2 * steps)),
-            dma((3, pieces)),
         ],
         compiler_params=pltpu.CompilerParams(
-            collective_id=0, has_side_effects=True, vmem_limit_bytes=62 << 20
+            collective_id=0, has_side_effects=True, vmem_limit_bytes=VMEM_LIMIT
         ),
         cost_estimate=pl.CostEstimate(flops=flops, bytes_accessed=20 << 20, transcendentals=0),
     )(block_rows, block_columns, tokens, targets, up_local, down_local)
+    new_up, new_down, input_grad = pl.pallas_call(
+        store_kernel,
+        out_shape=[jax.ShapeDtypeStruct(a.shape, a.dtype) for a in (new_up, new_down, input_grad)],
+        in_specs=[pl.BlockSpec(memory_space=vmem)] * 3,
+        out_specs=[anywhere] * 3,
+        scratch_shapes=[dma((3, STORES))],
+        compiler_params=pltpu.CompilerParams(vmem_limit_bytes=1 << 20),
+        cost_estimate=pl.CostEstimate(flops=0, bytes_accessed=10 << 20, transcendentals=0),
+    )(new_up, new_down, input_grad)
     return (new_up[None], new_down[None], input_grad)
 
 

time: 253 us -> 243 us (0.960)
  the two profiles are of different devices: /device:TPU:1 before, /device:TPU:32 now
where the time goes in v1:
time: 243 us
  Pallas kernels  243 us (100%)
    pallas_call x1, Pallas kernels, on_device(): pl.pallas_call(lambda *refs: step_kernel(apart, scale_in, scale_out, *ref...  240 us

profile of v1, /device:TPU:32, one launch (start us, length us, event | category | flops | bytes accessed | tf_op | source)
XLA Modules:
  0.0 243.2 jit_solution(9620423318079886382)
XLA Ops:
  0.6 240.2 %shard_map.85 = (bf16[16,256,256]{2,1,0:T(8,128)(2,1)S(1)}, bf16[16,256,256]{2,1,0:T(8,128)(2,1)S(1)}, bf16[768,512]{1,0:T(8,128)(2,1)S(1)}) custom-call(s32[16]{0:T(128)} %refs_0_.1, s32[16]{0:T(128)} %refs_1_.1, bf16[768,2048]{1,0:T(8,128)(2,1)} %refs_2_.1, bf16[768,2048]{1,0:T(8,128)(2,1)} %refs_3_.1, bf16[16,256,256]{2,1,0:T(8,128)(2,1)} %bitcast.4, ...), custom_call_target="tpu_custom_call" | custom-call | flops 9663676416 | bytes 20971520 | tf_op jit(solution)/shard_map/pallas_call | solution.py:369
  240.9 2.3 shard_map.86

commit v2 on v1

--- a/solution.py
+++ b/solution.py
@@ -15,7 +15,7 @@
 PIECE = 2
 VMEM_LIMIT = 54 << 20
 STORES = 4
-EARLY = (3, 3, 2)
+EARLY = (3, 5, 3)
 
 
 def dot(a, b, contract):
@@ -97,12 +97,11 @@
         pltpu.make_async_copy(down_hbm, down, load_sem.at[1]),
         pltpu.make_async_copy(target_hbm.at[pl.ds(aligned(mine), half)], target, load_sem.at[2]),
     ]
+    barrier = pltpu.get_barrier_semaphore()
+    for device in (partner, across, twin):
+        pl.semaphore_signal(barrier, inc=1, device_id=device, device_id_type=MESH)
     for load in loads:
         load.start()
-
-    barrier = pltpu.get_barrier_semaphore()
-    for device in (twin, across, partner):
-        pl.semaphore_signal(barrier, inc=1, device_id=device, device_id_type=MESH)
     pl.semaphore_wait(barrier, 3)
 
     def remote(src, dst, sems, where, device):

time: 243 us -> 243 us (level)
  no operation moved by 1% of the time
where the time goes in v2:
time: 243 us
  Pallas kernels  243 us (100%)
    pallas_call x1, Pallas kernels, on_device(): pl.pallas_call(lambda *refs: step_kernel(apart, scale_in, scale_out, *ref...  240 us

profile of v2, /device:TPU:32, one launch (start us, length us, event | category | flops | bytes accessed | tf_op | source)
XLA Modules:
  0.0 243.2 jit_solution(15769620720201427761)
XLA Ops:
  0.6 240.2 %shard_map.85 = (bf16[16,256,256]{2,1,0:T(8,128)(2,1)S(1)}, bf16[16,256,256]{2,1,0:T(8,128)(2,1)S(1)}, bf16[768,512]{1,0:T(8,128)(2,1)S(1)}) custom-call(s32[16]{0:T(128)} %refs_0_.1, s32[16]{0:T(128)} %refs_1_.1, bf16[768,2048]{1,0:T(8,128)(2,1)} %refs_2_.1, bf16[768,2048]{1,0:T(8,128)(2,1)} %refs_3_.1, bf16[16,256,256]{2,1,0:T(8,128)(2,1)} %bitcast.4, ...), custom_call_target="tpu_custom_call" | custom-call | flops 9663676416 | bytes 20971520 | tf_op jit(solution)/shard_map/pallas_call | solution.py:368
  240.9 2.3 shard_map.86

commit v3 on v2

--- a/solution.py
+++ b/solution.py
@@ -15,7 +15,7 @@
 PIECE = 2
 VMEM_LIMIT = 54 << 20
 STORES = 4
-EARLY = (3, 5, 3)
+EARLY = (4, 5, 3)
 
 
 def dot(a, b, contract):
@@ -64,12 +64,12 @@
 
 def step_kernel(
     apart, scale_in, scale_out,
-    rows_ref, cols_ref, tok_hbm, target_hbm, up_hbm, down_hbm,
+    rows_hbm, cols_hbm, tok_hbm, target_hbm, up_hbm, down_hbm,
     new_up, new_down, grad,
     tok, target, up, down, pre, act, dpre, seg, part, err_mine, err_other, gpart,
     out_twin, out_sum, out_across, grad_twin, grad_sum, grad_across,
     peer, down_half,
-    rank, col_block, col_row, row_block, row_col, row_row, keep, slot,
+    rows_ref, cols_ref, rank, col_block, col_row, row_block, row_col, row_row, keep, slot,
     load_sem, weight_sem, out_sem, grad_sem,
 ):
     hidden, tok_count, block = pre.shape
@@ -88,6 +88,10 @@
     def aligned(start):
         return pl.multiple_of(start, TILE)
 
+    tables = [
+        pltpu.make_async_copy(rows_hbm, rows_ref, load_sem.at[3 + model]),
+        pltpu.make_async_copy(cols_hbm, cols_ref, load_sem.at[4 + model]),
+    ]
     loads = [
         pltpu.make_async_copy(up_hbm, up, load_sem.at[0]),
         *(
@@ -100,7 +104,7 @@
     barrier = pltpu.get_barrier_semaphore()
     for device in (partner, across, twin):
         pl.semaphore_signal(barrier, inc=1, device_id=device, device_id_type=MESH)
-    for load in loads:
+    for load in tables + loads:
         load.start()
     pl.semaphore_wait(barrier, 3)
 
@@ -123,6 +127,8 @@
     cut = [sum(EARLY[: i + 1]) for i in range(3)]
     send_pieces(0, cut[0])
 
+    for table in tables:
+        table.wait()
     rank_blocks(cols_ref, rank)
     in_order(rank, lambda k: k, col_block)
     in_order(rank, lambda k: rows_ref[k], col_row)
@@ -362,13 +368,12 @@
     steps, pieces = half // TILE, blocks // PIECE
     vmem, dma = pltpu.VMEM, pltpu.SemaphoreType.DMA
     anywhere = pl.BlockSpec(memory_space=pl.ANY)
-    scalars = pl.BlockSpec(memory_space=pltpu.SMEM)
     weights = vmem((blocks, block, block), BF16)
     flops = 12 * tok_count * blocks * block * block
     new_up, new_down, input_grad = pl.pallas_call(
         lambda *refs: step_kernel(apart, scale_in, scale_out, *refs),
         out_shape=[weights, weights, vmem((tok_count, owned), BF16)],
-        in_specs=[scalars, scalars, anywhere, anywhere, anywhere, anywhere],
+        in_specs=[anywhere] * 6,
         out_specs=[pl.BlockSpec(memory_space=vmem)] * 3,
         scratch_shapes=[
             vmem((model, tok_count, block), BF16),
@@ -391,9 +396,9 @@
             vmem((tok_count, owned), BF16),
             vmem((2, blocks, block, block), BF16),
             vmem((blocks, block, block), F32),
-            *[pltpu.SMEM((blocks,), jnp.int32)] * 7,
+            *[pltpu.SMEM((blocks,), jnp.int32)] * 9,
             pltpu.SMEM((model,), jnp.int32),
-            dma((3 + model,)),
+            dma((5 + model,)),
             dma((2, 2, pieces)),
             dma((2, 3, steps)),
             dma((2, 3, 2 * steps)),

time: 243 us -> 243 us (level)
  no operation moved by 1% of the time
where the time goes in v3:
time: 243 us; the launch traced here: 242 us
  Pallas kernels  242 us (100%)
    pallas_call x1, Pallas kernels, on_device(): pl.pallas_call(lambda *refs: step_kernel(apart, scale_in, scale_out, *ref...  239 us

profile of v3, /device:TPU:32, one launch (start us, length us, event | category | flops | bytes accessed | tf_op | source)
XLA Modules:
  0.0 242.5 jit_solution(8405394380164548869)
XLA Ops:
  0.6 239.5 %shard_map.85 = (bf16[16,256,256]{2,1,0:T(8,128)(2,1)S(1)}, bf16[16,256,256]{2,1,0:T(8,128)(2,1)S(1)}, bf16[768,512]{1,0:T(8,128)(2,1)S(1)}) custom-call(s32[16]{0:T(128)} %refs_0_.1, s32[16]{0:T(128)} %refs_1_.1, bf16[768,2048]{1,0:T(8,128)(2,1)} %refs_2_.1, bf16[768,2048]{1,0:T(8,128)(2,1)} %refs_3_.1, bf16[16,256,256]{2,1,0:T(8,128)(2,1)} %bitcast.4, ...), custom_call_target="tpu_custom_call" | custom-call | flops 9663676416 | bytes 20971520 | tf_op jit(solution)/shard_map/pallas_call | solution.py:373
  240.1 2.3 shard_map.86

commit v4 on v3

--- a/solution.py
+++ b/solution.py
@@ -15,7 +15,7 @@
 PIECE = 2
 VMEM_LIMIT = 54 << 20
 STORES = 4
-EARLY = (4, 5, 3)
+EARLY = (5, 6, 2)
 
 
 def dot(a, b, contract):

time: 243 us -> 243 us (level)
  no operation moved by 1% of the time
where the time goes in v4:
time: 243 us
  Pallas kernels  242 us (100%)
    pallas_call x1, Pallas kernels, on_device(): pl.pallas_call(lambda *refs: step_kernel(apart, scale_in, scale_out, *ref...  240 us

profile of v4, /device:TPU:32, one launch (start us, length us, event | category | flops | bytes accessed | tf_op | source)
XLA Modules:
  0.0 242.5 jit_solution(4412684954864228218)
XLA Ops:
  0.6 239.6 %shard_map.85 = (bf16[16,256,256]{2,1,0:T(8,128)(2,1)S(1)}, bf16[16,256,256]{2,1,0:T(8,128)(2,1)S(1)}, bf16[768,512]{1,0:T(8,128)(2,1)S(1)}) custom-call(s32[16]{0:T(128)} %refs_0_.1, s32[16]{0:T(128)} %refs_1_.1, bf16[768,2048]{1,0:T(8,128)(2,1)} %refs_2_.1, bf16[768,2048]{1,0:T(8,128)(2,1)} %refs_3_.1, bf16[16,256,256]{2,1,0:T(8,128)(2,1)} %bitcast.4, ...), custom_call_target="tpu_custom_call" | custom-call | flops 9663676416 | bytes 20971520 | tf_op jit(solution)/shard_map/pallas_call | solution.py:373
  240.2 2.3 shard_map.86
